TPU v7x, 128 devices: a whole 4x4x4 slice. The times are simulated.
128 devices in a mesh: sx: 16 (over z, y), sy: 8 (over x, core).
Axes of the slice: x: 4, y: 4, z: 4, core: 2. Of those that a mesh axis runs over, the one named last changes fastest.
Arguments:
- obs_values: bfloat16 [32768, 64], P(('sx', 'sy')), may hold values from -6 to 6
- obs_dest: int32 [32768, 1], P(('sx', 'sy')), may hold values from 0 to 127; in each aligned block of 256 rows (0 to 255, 256 to 511, ...) at most 4 rows name the same one
- obs_node: int32 [32768], P(('sx', 'sy')), may hold values from 0 to 2047
- schur: bfloat16 [16, 8, 2048, 2048], P('sx', 'sy'), as said below
- local_inverse: bfloat16 [16, 8, 2048, 2048], P('sx', 'sy'), as said below
- coarse_inverse: float32 [1024, 1024], P(('sx', 'sy')), as said below
Outputs:
- solution_field: float32 [16, 8, 64, 2048], P('sx', 'sy')
- residual: float32 [16, 8, 64, 2048], P('sx', 'sy')
Inputs may be any that keep to these rules, and one draw needn't show every extreme that they name: `obs_dest`: at most 4 observations of one device go to one subdomain. `schur`: symmetric positive definite. `local_inverse`: symmetric positive definite. `coarse_inverse`: symmetric positive definite.
All inputs are finite; a program needn't handle non-finite values.
Results may differ from a plain program's by a relative error of at most 0.04.
Values may be sent and summed in bfloat16 or wider, within the bound.
A program may use at most 128 MiB of HBM per device.

v0:
```python
import jax
import jax.numpy as jnp
from jax import lax
from jax.sharding import PartitionSpec as P

ITERS = 6


def shortened(array):

    def short(part):
        return part.astype(jnp.bfloat16) if part.dtype == jnp.float32 else part

    return jax.tree.map(short, array)


def padded_2(cells, sides, width):
    for axis, dim in sides:
        count = lax.axis_size(axis)
        ends = count - 1
        head = lax.slice_in_dim(cells, 0, width, axis=dim)
        tail = lax.slice_in_dim(cells, cells.shape[dim] - width, cells.shape[dim], axis=dim)
        cells = jnp.concatenate(
            [
                lax.ppermute(tail, axis, [(i, (i + 1) % count) for i in range(ends)]),
                cells,
                lax.ppermute(head, axis, [((i + 1) % count, i) for i in range(ends)]),
            ],
            axis=dim,
        )
    return cells


def edge_weights(size):
    edge_len = size // 4
    col_index = lax.axis_index("sx")
    row_index = lax.axis_index("sy")
    col_count = lax.axis_size("sx")
    row_count = lax.axis_size("sy")
    sides = (
        jnp.where(col_index > 0, 0.5, 1.0),
        jnp.where(col_index < col_count - 1, 0.5, 1.0),
        jnp.where(row_index > 0, 0.5, 1.0),
        jnp.where(row_index < row_count - 1, 0.5, 1.0),
    )
    return jnp.concatenate([jnp.full((edge_len,), value, jnp.float32) for value in sides])


def coarse_basis(size, count):
    edge_len = size // 4
    node = jnp.arange(size)
    side = node // edge_len
    offset = (node % edge_len).astype(jnp.float32) - (edge_len - 1) / 2.0
    norm_ramp = jnp.sqrt(jnp.float32(edge_len * (edge_len * edge_len - 1) / 12.0))
    column = jnp.arange(count)
    on_edge = side[:, None] == (column // 2)[None, :]
    value = jnp.where(
        (column % 2 == 0)[None, :],
        1.0 / jnp.sqrt(jnp.float32(edge_len)),
        offset[:, None] / norm_ramp,
    )
    return jnp.where(on_edge, value, 0.0)


def assemble(local):
    edge_len = local.shape[1] // 4
    west_part = local[:, 0:edge_len]
    east_part = local[:, edge_len : 2 * edge_len]
    south_part = local[:, 2 * edge_len : 3 * edge_len]
    north_part = local[:, 3 * edge_len :]
    padded = padded_2(shortened(local[None, None]), (("sx", 0), ("sy", 1)), 1)
    west = west_part + padded[0, 1, :, edge_len : 2 * edge_len]
    east = east_part + padded[2, 1, :, 0:edge_len]
    south = south_part + padded[1, 0, :, 3 * edge_len :]
    north = north_part + padded[1, 2, :, 2 * edge_len : 3 * edge_len]
    return jnp.concatenate([west, east, south, north], axis=1)


def gather_coarse(coarse_local):
    return lax.all_gather(coarse_local, ("sx", "sy"), axis=0, tiled=True)


def body(obs_values, obs_dest, obs_node, schur, local_inverse, coarse_inverse):
    hp = lax.Precision.HIGHEST
    size = schur.shape[-1]
    count = coarse_inverse.shape[0]
    realiz = obs_values.shape[1]
    obs_count = obs_values.shape[0]
    row_count = lax.axis_size("sy")
    dev_count = lax.axis_size("sx") * row_count
    target = obs_dest[:, 0]
    capacity = max(2, 2 * obs_count // dev_count)
    match_table = (target[:, None] == jnp.arange(dev_count)[None, :]).astype(jnp.int32)
    slot_index = jnp.sum(jnp.cumsum(match_table, axis=0) * match_table, axis=1) - 1
    position = target * capacity + slot_index
    send_values = (
        jnp.zeros((dev_count * capacity, realiz), jnp.bfloat16).at[position].set(obs_values)
    )
    send_nodes = jnp.zeros((dev_count * capacity,), jnp.int32).at[position].set(obs_node)
    got_values, got_nodes = (
        lax.all_to_all(
            send_values.reshape(dev_count, capacity, realiz),
            ("sx", "sy"),
            split_axis=0,
            concat_axis=0,
            tiled=True,
        ),
        lax.all_to_all(
            send_nodes.reshape(dev_count, capacity),
            ("sx", "sy"),
            split_axis=0,
            concat_axis=0,
            tiled=True,
        ),
    )
    load = jax.ops.segment_sum(
        got_values.reshape(-1, realiz).astype(jnp.float32), got_nodes.reshape(-1), num_segments=size
    )
    rhs = assemble(load.T)
    weight = edge_weights(size)[None, :]
    basis = coarse_basis(size, count)
    schur_mat = schur[0, 0]
    inverse_mat = local_inverse[0, 0]

    def project(vec):
        return jnp.dot(weight * vec, basis, precision=hp).T

    def precond(vec, coarse_all):
        scaled = weight * vec
        part = jnp.dot(scaled.astype(jnp.bfloat16), inverse_mat, preferred_element_type=jnp.float32)
        solved = jnp.dot(coarse_inverse, coarse_all, precision=hp)
        correction = jnp.dot(solved.T, basis.T, precision=hp)
        return assemble(weight * (part + correction))

    def products(left, right):
        return lax.psum(jnp.sum(weight * left * right, axis=1), ("sx", "sy"))

    solution_field = jnp.zeros_like(rhs)
    residual = rhs
    coarse_resid = gather_coarse(project(residual))
    precon = precond(residual, coarse_resid)
    direction = precon
    rz_now = products(residual, precon)
    for step in range(ITERS):
        image = assemble(
            jnp.dot(direction.astype(jnp.bfloat16), schur_mat, preferred_element_type=jnp.float32)
        )
        curv_local = jnp.sum(weight * direction * image, axis=1)
        curv = lax.psum(curv_local, ("sx", "sy"))
        alpha = rz_now / curv
        solution_field = solution_field + alpha[:, None] * direction
        residual = residual - alpha[:, None] * image
        if step < ITERS - 1:
            coarse_resid = gather_coarse(project(residual))
            precon = precond(residual, coarse_resid)
            rz_next = products(residual, precon)
            direction = precon + (rz_next / rz_now)[:, None] * direction
            rz_now = rz_next
    return (solution_field[None, None], residual[None, None])


def solution(mesh):
    placed = (
        P(("sx", "sy"), None),
        P(("sx", "sy"), None),
        P(("sx", "sy")),
        P("sx", "sy", None, None),
        P("sx", "sy", None, None),
        P(("sx", "sy"), None),
    )
    return jax.shard_map(
        body,
        mesh=mesh,
        in_specs=placed,
        out_specs=(P("sx", "sy", None, None), P("sx", "sy", None, None)),
        check_vma=False,
    )
```

profile of v0, /device:TPU:1, one launch (start us, length us, event | category | flops | bytes accessed | tf_op | source)
XLA Modules:
  0.0 1432.0 jit_solution(6117860953516433841)
XLA Ops:
  5.6 11.5 all-to-all-start
  19.9 6.7 all-to-all-done
  26.6 4.5 all-to-all-start.1
  32.6 8.1 all-to-all-done.1
  45.1 4.0 collective-permute-start
  60.7 7.6 collective-permute-done.3
  72.7 39.9 %all_gather.18 = f32[1024,64]{1,0:T(8,128)S(1)} all-gather(f32[8,64]{1,0:T(8,128)S(1)} %fusion.35), channel_id=1, replica_groups=mesh['sx'=16,'sy'=8] {'sx','sy'}, dimensions={0}, use_global_device_ids=true | all-gather | bytes 264192 | tf_op jit(solution)/shard_map/all_gather | solution.py:80
  112.6 5.1 fusion.22
  125.1 4.3 collective-permute-done.5
  136.0 7.7 collective-permute-done.7
  147.9 4.8 collective-permute-start.8
  158.0 5.3 collective-permute-start.10
  163.3 7.7 collective-permute-done.11
  172.5 69.8 %all-reduce = (f32[64]{0:T(128)S(1)}, f32[64]{0:T(128)S(1)}) all-reduce(f32[64]{0:T(128)S(1)} %get-tuple-element.3, f32[64]{0:T(128)S(1)} %get-tuple-element.2), channel_id=1, replica_groups=mesh['sx'=16,'sy'=8] {'sx','sy'}, use_global_device_ids=true, to_apply=%region_7.8 | all-reduce | flops 128 | bytes 1024 | tf_op jit(solution)/shard_map/psum | solution.py:136
  244.8 5.0 fusion.20
  249.8 34.5 %all_gather.19 = f32[1024,64]{1,0:T(8,128)S(1)} all-gather(f32[8,64]{1,0:T(8,128)S(1)} %fusion.34), channel_id=1, replica_groups=mesh['sx'=16,'sy'=8] {'sx','sy'}, dimensions={0}, use_global_device_ids=true | all-gather | bytes 264192 | tf_op jit(solution)/shard_map/all_gather | solution.py:80
  287.7 4.0 collective-permute-start.12
  291.7 4.3 collective-permute-done.13
  302.5 7.7 collective-permute-done.15
  311.7 67.8 %psum.86 = f32[64]{0:T(128)S(1)} all-reduce(f32[64]{0:T(128)S(1)} %multiply_reduce_fusion.8), channel_id=1, replica_groups=mesh['sx'=16,'sy'=8] {'sx','sy'}, use_global_device_ids=true, to_apply=%region_11.12 | all-reduce | flops 64 | bytes 512 | tf_op jit(solution)/shard_map/psum | solution.py:136
  379.7 4.9 fusion.8
  394.3 4.2 collective-permute-start.19
  400.4 7.4 collective-permute-done.19
  409.6 68.1 %psum.87 = f32[64]{0:T(128)S(1)} all-reduce(f32[64]{0:T(128)S(1)} %multiply_reduce_fusion.7), channel_id=1, replica_groups=mesh['sx'=16,'sy'=8] {'sx','sy'}, use_global_device_ids=true, to_apply=%region_13.14 | all-reduce | flops 64 | bytes 512 | tf_op jit(solution)/shard_map/psum | solution.py:149
  480.2 4.9 fusion.18
  485.2 34.6 %all_gather.20 = f32[1024,64]{1,0:T(8,128)S(1)} all-gather(f32[8,64]{1,0:T(8,128)S(1)} %fusion.33), channel_id=1, replica_groups=mesh['sx'=16,'sy'=8] {'sx','sy'}, dimensions={0}, use_global_device_ids=true | all-gather | bytes 264192 | tf_op jit(solution)/shard_map/all_gather | solution.py:80
  523.1 4.0 collective-permute-start.20
  527.1 4.3 collective-permute-done.21
  538.0 7.7 collective-permute-done.23
  547.9 68.0 %psum.88 = f32[64]{0:T(128)S(1)} all-reduce(f32[64]{0:T(128)S(1)} %multiply_reduce_fusion.6), channel_id=1, replica_groups=mesh['sx'=16,'sy'=8] {'sx','sy'}, use_global_device_ids=true, to_apply=%region_15.16 | all-reduce | flops 64 | bytes 512 | tf_op jit(solution)/shard_map/psum | solution.py:136
  617.1 4.9 fusion.6
  623.4 4.0 collective-permute-start.24
  631.7 4.2 collective-permute-start.27
  637.8 7.3 collective-permute-done.27
  647.0 68.1 %psum.89 = f32[64]{0:T(128)S(1)} all-reduce(f32[64]{0:T(128)S(1)} %multiply_reduce_fusion.5), channel_id=1, replica_groups=mesh['sx'=16,'sy'=8] {'sx','sy'}, use_global_device_ids=true, to_apply=%region_17.18 | all-reduce | flops 64 | bytes 512 | tf_op jit(solution)/shard_map/psum | solution.py:149
  718.6 5.0 fusion.16
  723.6 34.8 %all_gather.21 = f32[1024,64]{1,0:T(8,128)S(1)} all-gather(f32[8,64]{1,0:T(8,128)S(1)} %fusion.32), channel_id=1, replica_groups=mesh['sx'=16,'sy'=8] {'sx','sy'}, dimensions={0}, use_global_device_ids=true | all-gather | bytes 264192 | tf_op jit(solution)/shard_map/all_gather | solution.py:80
  765.7 4.3 collective-permute-done.29
  776.6 7.7 collective-permute-done.31
  785.8 68.0 %psum.90 = f32[64]{0:T(128)S(1)} all-reduce(f32[64]{0:T(128)S(1)} %multiply_reduce_fusion.4), channel_id=1, replica_groups=mesh['sx'=16,'sy'=8] {'sx','sy'}, use_global_device_ids=true, to_apply=%region_19.20 | all-reduce | flops 64 | bytes 512 | tf_op jit(solution)/shard_map/psum | solution.py:136
  854.0 4.9 fusion.4
  868.5 4.2 collective-permute-start.35
  874.7 7.3 collective-permute-done.35
  883.9 68.1 %psum.91 = f32[64]{0:T(128)S(1)} all-reduce(f32[64]{0:T(128)S(1)} %multiply_reduce_fusion.3), channel_id=1, replica_groups=mesh['sx'=16,'sy'=8] {'sx','sy'}, use_global_device_ids=true, to_apply=%region_21.22 | all-reduce | flops 64 | bytes 512 | tf_op jit(solution)/shard_map/psum | solution.py:149
  954.4 5.0 fusion.14
  959.4 34.5 %all_gather.22 = f32[1024,64]{1,0:T(8,128)S(1)} all-gather(f32[8,64]{1,0:T(8,128)S(1)} %fusion.31), channel_id=1, replica_groups=mesh['sx'=16,'sy'=8] {'sx','sy'}, dimensions={0}, use_global_device_ids=true | all-gather | bytes 264192 | tf_op jit(solution)/shard_map/all_gather | solution.py:80
  997.3 4.0 collective-permute-start.36
  1001.3 4.3 collective-permute-done.37
  1012.2 7.7 collective-permute-done.39
  1022.2 68.0 %psum.92 = f32[64]{0:T(128)S(1)} all-reduce(f32[64]{0:T(128)S(1)} %multiply_reduce_fusion.2), channel_id=1, replica_groups=mesh['sx'=16,'sy'=8] {'sx','sy'}, use_global_device_ids=true, to_apply=%region_23.24 | all-reduce | flops 64 | bytes 512 | tf_op jit(solution)/shard_map/psum | solution.py:136
  1091.4 4.9 fusion.2
  1106.0 4.2 collective-permute-start.43
  1112.1 7.3 collective-permute-done.43
  1121.3 68.1 %psum.93 = f32[64]{0:T(128)S(1)} all-reduce(f32[64]{0:T(128)S(1)} %multiply_reduce_fusion.1), channel_id=1, replica_groups=mesh['sx'=16,'sy'=8] {'sx','sy'}, use_global_device_ids=true, to_apply=%region_25.26 | all-reduce | flops 64 | bytes 512 | tf_op jit(solution)/shard_map/psum | solution.py:149
  1191.8 5.0 fusion.12
  1196.8 34.6 %all_gather.23 = f32[1024,64]{1,0:T(8,128)S(1)} all-gather(f32[8,64]{1,0:T(8,128)S(1)} %fusion.30), channel_id=1, replica_groups=mesh['sx'=16,'sy'=8] {'sx','sy'}, dimensions={0}, use_global_device_ids=true | all-gather | bytes 264192 | tf_op jit(solution)/shard_map/all_gather | solution.py:80
  1234.7 4.0 collective-permute-start.44
  1238.8 4.3 collective-permute-done.45
  1249.6 7.7 collective-permute-done.47
  1258.8 68.0 %psum.94 = f32[64]{0:T(128)S(1)} all-reduce(f32[64]{0:T(128)S(1)} %multiply_reduce_fusion), channel_id=1, replica_groups=mesh['sx'=16,'sy'=8] {'sx','sy'}, use_global_device_ids=true, to_apply=%region_27.28 | all-reduce | flops 64 | bytes 512 | tf_op jit(solution)/shard_map/psum | solution.py:136
  1326.8 5.0 fusion
  1341.5 4.2 collective-permute-start.51
  1347.6 7.3 collective-permute-done.51
  1357.7 68.1 %psum.95 = f32[64]{0:T(128)S(1)} all-reduce(f32[64]{0:T(128)S(1)} %fusion.48), channel_id=1, replica_groups=mesh['sx'=16,'sy'=8] {'sx','sy'}, use_global_device_ids=true, to_apply=%region_29.30 | all-reduce | flops 64 | bytes 512 | tf_op jit(solution)/shard_map/psum | solution.py:149
  (284 shorter events, 201.6 us)
Async XLA Ops:
  0.6 117.1 %copy-start = (f32[8,1024]{1,0:T(8,128)S(1)}, f32[8,1024]{1,0:T(8,128)}, u32[]{:S(2)}) copy-start(f32[8,1024]{1,0:T(8,128)} %param.11) | copy-start | bytes 98308
  5.6 21.0 %all-to-all-start = ((s32[128,1,4]{2,1,0:T(1,128)}), s32[128,1,4]{2,1,0:T(1,128)S(1)}, u32[]{:S(2)}, u32[]{:S(2)}) async-start(s32[128,1,4]{2,1,0:T(1,128)} %bitcast.7), calls=%async_computation | async-start | bytes 131072 | tf_op jit(solution)/shard_map/all_to_all | solution.py:108
  26.6 14.0 all-to-all-start.1
  43.8 9.0 collective-permute-start.1
  45.1 8.5 collective-permute-start
  53.7 14.6 %collective-permute-start.3 = (bf16[3,1,64,2048]{3,2,1,0:T(8,128)(2,1)S(1)}, bf16[3,1,64,2048]{3,2,1,0:T(8,128)(2,1)S(1)}, u32[]{:S(2)}, u32[]{:S(2)}) collective-permute-start(bf16[3,1,64,2048]{3,2,1,0:T(8,128)(2,1)S(1)} %pad_maximum_fusion), channel_id=1, source_target_pairs={{1,0},{2,1},{3,2},{4,3},{5,4},{6,5},{7,6},{9,8},{10,9},{11,10},{12... | collective-permute-start | bytes 2359304 | tf_op jit(solution)/shard_map/ppermute | solution.py:27
  57.6 11.9 collective-permute-start.2
  119.8 9.6 collective-permute-start.5
  121.1 9.2 collective-permute-start.4
  130.4 13.3 collective-permute-start.7
  133.6 11.3 collective-permute-start.6
  146.6 7.9 collective-permute-start.9
  147.9 8.0 collective-permute-start.8
  156.1 15.0 %collective-permute-start.11 = (bf16[3,1,64,2048]{3,2,1,0:T(8,128)(2,1)S(1)}, bf16[3,1,64,2048]{3,2,1,0:T(8,128)(2,1)S(1)}, u32[]{:S(2)}, u32[]{:S(2)}) collective-permute-start(bf16[3,1,64,2048]{3,2,1,0:T(8,128)(2,1)S(1)} %pad_maximum_fusion.2), channel_id=1, source_target_pairs={{1,0},{2,1},{3,2},{4,3},{5,4},{6,5},{7,6},{9,8},{10,9},{11,10},{12... | collective-permute-start | bytes 2359304 | tf_op jit(solution)/shard_map/ppermute | solution.py:27
  158.0 14.2 collective-permute-start.10
  286.4 9.6 collective-permute-start.13
  287.7 9.2 collective-permute-start.12
  297.0 13.3 collective-permute-start.15
  300.2 11.3 collective-permute-start.14
  384.7 8.6 collective-permute-start.17
  386.0 8.2 collective-permute-start.16
  394.3 13.5 collective-permute-start.19
  398.5 10.8 collective-permute-start.18
  521.8 9.6 collective-permute-start.21
  523.1 9.2 collective-permute-start.20
  532.4 13.3 collective-permute-start.23
  535.6 11.3 collective-permute-start.22
  622.1 8.6 collective-permute-start.25
  623.4 8.2 collective-permute-start.24
  631.7 13.4 collective-permute-start.27
  635.9 10.8 collective-permute-start.26
  760.4 9.6 collective-permute-start.29
  761.7 9.2 collective-permute-start.28
  771.0 13.3 collective-permute-start.31
  774.2 11.3 collective-permute-start.30
  858.9 8.6 collective-permute-start.33
  860.2 8.2 collective-permute-start.32
  868.5 13.4 collective-permute-start.35
  872.8 10.8 collective-permute-start.34
  883.7 75.7 %copy-start.27 = (f32[64,512]{1,0:T(8,128)}, f32[64,512]{1,0:T(8,128)S(1)}, u32[]{:S(2)}) copy-start(f32[64,512]{1,0:T(8,128)S(1)} %get-tuple-element.22) | copy-start | bytes 393220
  996.0 9.6 collective-permute-start.37
  997.3 9.2 collective-permute-start.36
  1006.6 13.3 collective-permute-start.39
  1009.8 11.3 collective-permute-start.38
  1096.4 8.6 collective-permute-start.41
  1097.7 8.2 collective-permute-start.40
  1106.0 13.4 collective-permute-start.43
  1110.2 10.8 collective-permute-start.42
  1121.1 75.7 %copy-start.35 = (f32[64,512]{1,0:T(8,128)}, f32[64,512]{1,0:T(8,128)S(1)}, u32[]{:S(2)}) copy-start(f32[64,512]{1,0:T(8,128)S(1)} %get-tuple-element.14) | copy-start | bytes 393220
  1121.1 75.7 %copy-start.36 = (f32[64,512]{1,0:T(8,128)}, f32[64,512]{1,0:T(8,128)S(1)}, u32[]{:S(2)}) copy-start(f32[64,512]{1,0:T(8,128)S(1)} %get-tuple-element.15) | copy-start | bytes 393220
  1121.1 75.7 %copy-start.37 = (f32[64,512]{1,0:T(8,128)}, f32[64,512]{1,0:T(8,128)S(1)}, u32[]{:S(2)}) copy-start(f32[64,512]{1,0:T(8,128)S(1)} %get-tuple-element.16) | copy-start | bytes 393220
  1121.1 75.7 %copy-start.38 = (f32[64,512]{1,0:T(8,128)}, f32[64,512]{1,0:T(8,128)S(1)}, u32[]{:S(2)}) copy-start(f32[64,512]{1,0:T(8,128)S(1)} %get-tuple-element.17) | copy-start | bytes 393220
  1233.4 9.6 collective-permute-start.45
  1234.7 9.2 collective-permute-start.44
  1244.0 13.3 collective-permute-start.47
  1247.2 11.3 collective-permute-start.46
  1258.6 167.2 %copy-start.6 = (f32[64,512]{1,0:T(8,128)S(1)}, f32[64,512]{1,0:T(8,128)}, u32[]{:S(2)}) copy-start(f32[64,512]{1,0:T(8,128)} %copy-done.5) | copy-start | bytes 393220
  1258.6 167.2 %copy-start.8 = (f32[64,512]{1,0:T(8,128)S(1)}, f32[64,512]{1,0:T(8,128)}, u32[]{:S(2)}) copy-start(f32[64,512]{1,0:T(8,128)} %copy-done.7) | copy-start | bytes 393220
  1326.8 101.9 %copy-start.2 = (f32[64,512]{1,0:T(8,128)S(1)}, f32[64,512]{1,0:T(8,128)}, u32[]{:S(2)}) copy-start(f32[64,512]{1,0:T(8,128)} %copy-done.1) | copy-start | bytes 393220
  1326.8 101.9 %copy-start.4 = (f32[64,512]{1,0:T(8,128)S(1)}, f32[64,512]{1,0:T(8,128)}, u32[]{:S(2)}) copy-start(f32[64,512]{1,0:T(8,128)} %copy-done.3) | copy-start | bytes 393220
  1331.9 8.6 collective-permute-start.49
  1333.2 8.2 collective-permute-start.48
  1341.5 13.5 collective-permute-start.51
  1345.7 10.8 collective-permute-start.50
  (35 other events, 1586.3 us)
where the time goes:
time: 1440 us; the launch traced here: 1430 us
  blocking collectives  963 us (67%)
  waiting for transfers between devices  190 us (13%)
  starting transfers between devices  164 us (11%)
  matrix products  82.1 us (6%)
  other arithmetic  20.9 us (1%)
    psum x6, blocking collectives, products(): return lax.psum(jnp.sum(weight * left * right, axis=1), ('sx', 'sy'))  410 us
    psum x5, blocking collectives, body(): curv = lax.psum(curv_local, ('sx', 'sy'))  340 us
    all_gather x6, blocking collectives, gather_coarse(): return lax.all_gather(coarse_local, ('sx', 'sy'), axis=0, tiled=True)  213 us
    ppermute x26, waiting for transfers between devices, padded_2(): lax.ppermute(head, axis, [((i + 1) % count, i) for i in range(ends)])  146 us
    ppermute x26, starting transfers between devices, padded_2(): lax.ppermute(tail, axis, [(i, (i + 1) % count) for i in range(ends)])  84.9 us
    ppermute x26, starting transfers between devices, padded_2(): lax.ppermute(head, axis, [((i + 1) % count, i) for i in range(ends)])  62.8 us
    dot_general x6, matrix products, precond(): jnp.dot(scaled.astype(jnp.bfloat16), inverse_mat, preferred_element_type=...  29.9 us
    ppermute x26, waiting for transfers between devices, padded_2(): lax.ppermute(tail, axis, [(i, (i + 1) % count) for i in range(ends)])  29.5 us
  transfers between devices with their start and end apart: 54, of which 54 were waited for; matrix products, arithmetic and copies ran while one was open for 0% of the time, Pallas kernels for 0%

commit v1 on v0

--- a/solution.py
+++ b/solution.py
@@ -133,7 +133,7 @@
         return assemble(weight * (part + correction))
 
     def products(left, right):
-        return lax.psum(jnp.sum(weight * left * right, axis=1), ("sx", "sy"))
+        return lax.psum(lax.psum(jnp.sum(weight * left * right, axis=1), "sy"), "sx")
 
     solution_field = jnp.zeros_like(rhs)
     residual = rhs

time: 1440 us -> 1380 us (0.958)
  blocking collectives: 963 us -> 878 us
  starting transfers between devices: 164 us -> 195 us
    psum x6 -> x12, blocking collectives: 410 us -> 268 us  [the longest x6 195 us: products(): lax.psum(lax.psum(jnp.sum(weight * left * right, axis=1), 'sy'), 'sx')]
    psum x5 -> x6, blocking collectives: 340 us -> 391 us  [body(): curv = lax.psum(curv_local, ('sx', 'sy'))]
    ppermute x26, starting transfers between devices: 62.8 us -> 93.9 us  [padded_2(): lax.ppermute(head, axis, [((i + 1) % count, i) for i in range(ends)])]
where the time goes in v1:
time: 1380 us; the launch traced here: 1370 us
  blocking collectives  878 us (64%)
  starting transfers between devices  195 us (14%)
  waiting for transfers between devices  186 us (13%)
  matrix products  82.1 us (6%)
  other arithmetic  20.9 us (2%)
    psum x6, blocking collectives, body(): curv = lax.psum(curv_local, ('sx', 'sy'))  391 us
    all_gather x6, blocking collectives, gather_coarse(): return lax.all_gather(coarse_local, ('sx', 'sy'), axis=0, tiled=True)  219 us
    psum x6, blocking collectives, products(): lax.psum(lax.psum(jnp.sum(weight * left * right, axis=1), 'sy'), 'sx')  195 us
    ppermute x26, waiting for transfers between devices, padded_2(): lax.ppermute(head, axis, [((i + 1) % count, i) for i in range(ends)])  138 us
    ppermute x26, starting transfers between devices, padded_2(): lax.ppermute(head, axis, [((i + 1) % count, i) for i in range(ends)])  93.9 us
    ppermute x26, starting transfers between devices, padded_2(): lax.ppermute(tail, axis, [(i, (i + 1) % count) for i in range(ends)])  84.9 us
    psum x6, blocking collectives, products(): lax.psum(jnp.sum(weight * left * right, axis=1), 'sy')  72.7 us
    ppermute x26, waiting for transfers between devices, padded_2(): lax.ppermute(tail, axis, [(i, (i + 1) % count) for i in range(ends)])  33.7 us
  transfers between devices with their start and end apart: 54, of which 54 were waited for; matrix products, arithmetic and copies ran while one was open for 0% of the time, Pallas kernels for 0%

profile of v1, /device:TPU:1, one launch (start us, length us, event | category | flops | bytes accessed | tf_op | source)
XLA Modules:
  0.0 1373.6 jit_solution(11352750951777284190)
XLA Ops:
  5.6 11.5 all-to-all-start
  19.9 6.7 all-to-all-done
  26.6 4.5 all-to-all-start.1
  32.6 8.1 all-to-all-done.1
  60.7 7.6 collective-permute-done.3
  72.7 39.9 %all_gather.18 = f32[1024,64]{1,0:T(8,128)S(1)} all-gather(f32[8,64]{1,0:T(8,128)S(1)} %fusion.35), channel_id=1, replica_groups=mesh['sx'=16,'sy'=8] {'sx','sy'}, dimensions={0}, use_global_device_ids=true | all-gather | bytes 264192 | tf_op jit(solution)/shard_map/all_gather | solution.py:80
  112.6 5.1 fusion.22
  125.1 4.3 collective-permute-done.5
  136.0 7.7 collective-permute-done.7
  147.9 4.8 collective-permute-start.8
  158.0 5.3 collective-permute-start.10
  163.3 7.7 collective-permute-done.11
  172.5 69.9 %psum.128 = f32[64]{0:T(128)S(1)} all-reduce(f32[64]{0:T(128)S(1)} %get-tuple-element.2), channel_id=1, replica_groups=mesh['sx'=16,'sy'=8] {'sx','sy'}, use_global_device_ids=true, to_apply=%region_10.11 | all-reduce | flops 64 | bytes 512 | tf_op jit(solution)/shard_map/psum | solution.py:149
  242.4 12.7 psum.126
  255.1 30.6 %psum.127 = f32[64]{0:T(128)S(1)} all-reduce(f32[64]{0:T(128)S(1)} %psum.126), channel_id=1, replica_groups=mesh['sx'=16,'sy'=8] {'sx'}, use_global_device_ids=true, to_apply=%region_8.9 | all-reduce | flops 64 | bytes 512 | tf_op jit(solution)/shard_map/psum | solution.py:136
  288.1 5.0 fusion.20
  293.1 40.6 %all_gather.19 = f32[1024,64]{1,0:T(8,128)S(1)} all-gather(f32[8,64]{1,0:T(8,128)S(1)} %fusion.34), channel_id=1, replica_groups=mesh['sx'=16,'sy'=8] {'sx','sy'}, dimensions={0}, use_global_device_ids=true | all-gather | bytes 264192 | tf_op jit(solution)/shard_map/all_gather | solution.py:80
  341.0 4.3 collective-permute-done.13
  351.9 7.7 collective-permute-done.15
  361.1 12.8 psum.129
  373.8 33.1 %psum.130 = f32[64]{0:T(128)S(1)} all-reduce(f32[64]{0:T(128)S(1)} %psum.129), channel_id=1, replica_groups=mesh['sx'=16,'sy'=8] {'sx'}, use_global_device_ids=true, to_apply=%region_13.14 | all-reduce | flops 64 | bytes 512 | tf_op jit(solution)/shard_map/psum | solution.py:136
  407.1 4.9 fusion.8
  420.7 10.4 collective-permute-start.19
  433.1 7.0 collective-permute-done.19
  442.3 64.2 %psum.131 = f32[64]{0:T(128)S(1)} all-reduce(f32[64]{0:T(128)S(1)} %multiply_reduce_fusion.7), channel_id=1, replica_groups=mesh['sx'=16,'sy'=8] {'sx','sy'}, use_global_device_ids=true, to_apply=%region_15.16 | all-reduce | flops 64 | bytes 512 | tf_op jit(solution)/shard_map/psum | solution.py:149
  509.0 4.9 fusion.18
  514.0 34.6 %all_gather.20 = f32[1024,64]{1,0:T(8,128)S(1)} all-gather(f32[8,64]{1,0:T(8,128)S(1)} %fusion.33), channel_id=1, replica_groups=mesh['sx'=16,'sy'=8] {'sx','sy'}, dimensions={0}, use_global_device_ids=true | all-gather | bytes 264192 | tf_op jit(solution)/shard_map/all_gather | solution.py:80
  555.9 4.3 collective-permute-done.21
  566.7 7.7 collective-permute-done.23
  576.7 11.8 psum.132
  588.5 32.9 %psum.133 = f32[64]{0:T(128)S(1)} all-reduce(f32[64]{0:T(128)S(1)} %psum.132), channel_id=1, replica_groups=mesh['sx'=16,'sy'=8] {'sx'}, use_global_device_ids=true, to_apply=%region_18.19 | all-reduce | flops 64 | bytes 512 | tf_op jit(solution)/shard_map/psum | solution.py:136
  622.6 4.9 fusion.6
  636.3 10.4 collective-permute-start.27
  648.7 7.0 collective-permute-done.27
  657.9 64.2 %psum.134 = f32[64]{0:T(128)S(1)} all-reduce(f32[64]{0:T(128)S(1)} %multiply_reduce_fusion.5), channel_id=1, replica_groups=mesh['sx'=16,'sy'=8] {'sx','sy'}, use_global_device_ids=true, to_apply=%region_20.21 | all-reduce | flops 64 | bytes 512 | tf_op jit(solution)/shard_map/psum | solution.py:149
  725.7 5.0 fusion.16
  730.6 34.8 %all_gather.21 = f32[1024,64]{1,0:T(8,128)S(1)} all-gather(f32[8,64]{1,0:T(8,128)S(1)} %fusion.32), channel_id=1, replica_groups=mesh['sx'=16,'sy'=8] {'sx','sy'}, dimensions={0}, use_global_device_ids=true | all-gather | bytes 264192 | tf_op jit(solution)/shard_map/all_gather | solution.py:80
  783.6 7.7 collective-permute-done.31
  792.8 11.8 psum.135
  804.6 33.0 %psum.136 = f32[64]{0:T(128)S(1)} all-reduce(f32[64]{0:T(128)S(1)} %psum.135), channel_id=1, replica_groups=mesh['sx'=16,'sy'=8] {'sx'}, use_global_device_ids=true, to_apply=%region_23.24 | all-reduce | flops 64 | bytes 512 | tf_op jit(solution)/shard_map/psum | solution.py:136
  837.7 4.9 fusion.4
  851.4 10.4 collective-permute-start.35
  863.8 7.0 collective-permute-done.35
  873.0 64.2 %psum.137 = f32[64]{0:T(128)S(1)} all-reduce(f32[64]{0:T(128)S(1)} %multiply_reduce_fusion.3), channel_id=1, replica_groups=mesh['sx'=16,'sy'=8] {'sx','sy'}, use_global_device_ids=true, to_apply=%region_25.26 | all-reduce | flops 64 | bytes 512 | tf_op jit(solution)/shard_map/psum | solution.py:149
  939.6 5.0 fusion.14
  944.6 34.5 %all_gather.22 = f32[1024,64]{1,0:T(8,128)S(1)} all-gather(f32[8,64]{1,0:T(8,128)S(1)} %fusion.31), channel_id=1, replica_groups=mesh['sx'=16,'sy'=8] {'sx','sy'}, dimensions={0}, use_global_device_ids=true | all-gather | bytes 264192 | tf_op jit(solution)/shard_map/all_gather | solution.py:80
  986.5 4.3 collective-permute-done.37
  997.4 7.7 collective-permute-done.39
  1007.3 11.8 psum.138
  1019.1 32.9 %psum.139 = f32[64]{0:T(128)S(1)} all-reduce(f32[64]{0:T(128)S(1)} %psum.138), channel_id=1, replica_groups=mesh['sx'=16,'sy'=8] {'sx'}, use_global_device_ids=true, to_apply=%region_28.29 | all-reduce | flops 64 | bytes 512 | tf_op jit(solution)/shard_map/psum | solution.py:136
  1053.3 4.9 fusion.2
  1067.0 10.4 collective-permute-start.43
  1079.4 7.0 collective-permute-done.43
  1088.6 64.2 %psum.140 = f32[64]{0:T(128)S(1)} all-reduce(f32[64]{0:T(128)S(1)} %multiply_reduce_fusion.1), channel_id=1, replica_groups=mesh['sx'=16,'sy'=8] {'sx','sy'}, use_global_device_ids=true, to_apply=%region_30.31 | all-reduce | flops 64 | bytes 512 | tf_op jit(solution)/shard_map/psum | solution.py:149
  1155.2 5.0 fusion.12
  1160.3 34.6 %all_gather.23 = f32[1024,64]{1,0:T(8,128)S(1)} all-gather(f32[8,64]{1,0:T(8,128)S(1)} %fusion.30), channel_id=1, replica_groups=mesh['sx'=16,'sy'=8] {'sx','sy'}, dimensions={0}, use_global_device_ids=true | all-gather | bytes 264192 | tf_op jit(solution)/shard_map/all_gather | solution.py:80
  1202.2 4.3 collective-permute-done.45
  1213.0 7.7 collective-permute-done.47
  1222.2 11.8 psum.141
  1234.0 32.9 %psum.142 = f32[64]{0:T(128)S(1)} all-reduce(f32[64]{0:T(128)S(1)} %psum.141), channel_id=1, replica_groups=mesh['sx'=16,'sy'=8] {'sx'}, use_global_device_ids=true, to_apply=%region_33.34 | all-reduce | flops 64 | bytes 512 | tf_op jit(solution)/shard_map/psum | solution.py:136
  1267.0 5.0 fusion
  1280.8 10.4 collective-permute-start.51
  1293.1 7.1 collective-permute-done.51
  1303.2 64.2 %psum.143 = f32[64]{0:T(128)S(1)} all-reduce(f32[64]{0:T(128)S(1)} %fusion.48), channel_id=1, replica_groups=mesh['sx'=16,'sy'=8] {'sx','sy'}, use_global_device_ids=true, to_apply=%region_35.36 | all-reduce | flops 64 | bytes 512 | tf_op jit(solution)/shard_map/psum | solution.py:149
  (291 shorter events, 226.7 us)
Async XLA Ops:
  0.6 117.1 %copy-start = (f32[8,1024]{1,0:T(8,128)S(1)}, f32[8,1024]{1,0:T(8,128)}, u32[]{:S(2)}) copy-start(f32[8,1024]{1,0:T(8,128)} %param.11) | copy-start | bytes 98308
  5.6 21.0 %all-to-all-start = ((s32[128,1,4]{2,1,0:T(1,128)}), s32[128,1,4]{2,1,0:T(1,128)S(1)}, u32[]{:S(2)}, u32[]{:S(2)}) async-start(s32[128,1,4]{2,1,0:T(1,128)} %bitcast.7), calls=%async_computation | async-start | bytes 131072 | tf_op jit(solution)/shard_map/all_to_all | solution.py:108
  26.6 14.0 %all-to-all-start.1 = ((bf16[128,2,128]{2,1,0:T(2,128)(2,1)}), bf16[128,2,128]{2,1,0:T(2,128)(2,1)S(1)}, u32[]{:S(2)}, u32[]{:S(2)}) async-start(bf16[128,2,128]{2,1,0:T(2,128)(2,1)} %reshape.1414), calls=%async_computation.1 | async-start | bytes 131072 | tf_op jit(solution)/shard_map/all_to_all | solution.py:101
  43.8 9.0 collective-permute-start.1
  45.1 8.5 collective-permute-start
  53.7 14.6 %collective-permute-start.3 = (bf16[3,1,64,2048]{3,2,1,0:T(8,128)(2,1)S(1)}, bf16[3,1,64,2048]{3,2,1,0:T(8,128)(2,1)S(1)}, u32[]{:S(2)}, u32[]{:S(2)}) collective-permute-start(bf16[3,1,64,2048]{3,2,1,0:T(8,128)(2,1)S(1)} %pad_maximum_fusion), channel_id=1, source_target_pairs={{1,0},{2,1},{3,2},{4,3},{5,4},{6,5},{7,6},{9,8},{10,9},{11,10},{12... | collective-permute-start | bytes 2359304 | tf_op jit(solution)/shard_map/ppermute | solution.py:27
  57.6 11.9 collective-permute-start.2
  72.7 72.3 %slice-start = ((s8[8388608]{0:T(1024)(128)(4,1)}), s8[4194304]{0:T(1024)(128)(4,1)S(1)}, s32[]{:S(2)}) async-start(s8[8388608]{0:T(1024)(128)(4,1)} %bitcast.406), calls=%async_computation.2 | async-start | bytes 8388608
  119.8 9.6 collective-permute-start.5
  121.1 9.2 collective-permute-start.4
  130.4 13.3 collective-permute-start.7
  133.6 11.3 collective-permute-start.6
  146.6 7.9 collective-permute-start.9
  147.9 8.0 collective-permute-start.8
  156.1 15.0 %collective-permute-start.11 = (bf16[3,1,64,2048]{3,2,1,0:T(8,128)(2,1)S(1)}, bf16[3,1,64,2048]{3,2,1,0:T(8,128)(2,1)S(1)}, u32[]{:S(2)}, u32[]{:S(2)}) collective-permute-start(bf16[3,1,64,2048]{3,2,1,0:T(8,128)(2,1)S(1)} %pad_maximum_fusion.2), channel_id=1, source_target_pairs={{1,0},{2,1},{3,2},{4,3},{5,4},{6,5},{7,6},{9,8},{10,9},{11,10},{12... | collective-permute-start | bytes 2359304 | tf_op jit(solution)/shard_map/ppermute | solution.py:27
  158.0 14.2 %collective-permute-start.10 = (bf16[3,1,64,2048]{3,2,1,0:T(8,128)(2,1)S(1)}, bf16[3,1,64,2048]{3,2,1,0:T(8,128)(2,1)S(1)}, u32[]{:S(2)}, u32[]{:S(2)}) collective-permute-start(bf16[3,1,64,2048]{3,2,1,0:T(8,128)(2,1)S(1)} %pad_maximum_fusion.2), channel_id=1, source_target_pairs={{0,1},{1,2},{2,3},{3,4},{4,5},{5,6},{6,7},{8,9},{9,10},{10,11},{11... | collective-permute-start | bytes 2359304 | tf_op jit(solution)/shard_map/ppermute | solution.py:25
  172.3 115.8 %copy-start.1 = (f32[64,512]{1,0:T(8,128)}, f32[64,512]{1,0:T(8,128)S(1)}, u32[]{:S(2)}) copy-start(f32[64,512]{1,0:T(8,128)S(1)} %get-tuple-element.46) | copy-start | bytes 393220
  172.3 115.8 %copy-start.3 = (f32[64,512]{1,0:T(8,128)}, f32[64,512]{1,0:T(8,128)S(1)}, u32[]{:S(2)}) copy-start(f32[64,512]{1,0:T(8,128)S(1)} %get-tuple-element.47) | copy-start | bytes 393220
  335.7 9.6 collective-permute-start.13
  337.0 9.2 collective-permute-start.12
  346.3 13.3 collective-permute-start.15
  349.5 11.3 collective-permute-start.14
  412.1 7.1 collective-permute-start.17
  413.4 7.3 collective-permute-start.16
  420.7 19.4 %collective-permute-start.19 = (bf16[3,1,64,2048]{3,2,1,0:T(8,128)(2,1)S(1)}, bf16[3,1,64,2048]{3,2,1,0:T(8,128)(2,1)S(1)}, u32[]{:S(2)}, u32[]{:S(2)}) collective-permute-start(bf16[3,1,64,2048]{3,2,1,0:T(8,128)(2,1)S(1)} %pad_maximum_fusion.4), channel_id=1, source_target_pairs={{1,0},{2,1},{3,2},{4,3},{5,4},{6,5},{7,6},{9,8},{10,9},{11,10},{12... | collective-permute-start | bytes 2359304 | tf_op jit(solution)/shard_map/ppermute | solution.py:27
  431.2 10.8 collective-permute-start.18
  550.6 9.6 collective-permute-start.21
  551.9 9.2 collective-permute-start.20
  561.2 13.3 collective-permute-start.23
  564.4 11.3 collective-permute-start.22
  627.6 7.1 collective-permute-start.25
  628.9 7.3 collective-permute-start.24
  636.3 19.4 %collective-permute-start.27 = (bf16[3,1,64,2048]{3,2,1,0:T(8,128)(2,1)S(1)}, bf16[3,1,64,2048]{3,2,1,0:T(8,128)(2,1)S(1)}, u32[]{:S(2)}, u32[]{:S(2)}) collective-permute-start(bf16[3,1,64,2048]{3,2,1,0:T(8,128)(2,1)S(1)} %pad_maximum_fusion.6), channel_id=1, source_target_pairs={{1,0},{2,1},{3,2},{4,3},{5,4},{6,5},{7,6},{9,8},{10,9},{11,10},{12... | collective-permute-start | bytes 2359304 | tf_op jit(solution)/shard_map/ppermute | solution.py:27
  646.8 10.8 collective-permute-start.26
  767.4 9.6 collective-permute-start.29
  768.7 9.2 collective-permute-start.28
  778.0 13.3 collective-permute-start.31
  781.2 11.3 collective-permute-start.30
  842.7 7.1 collective-permute-start.33
  844.0 7.3 collective-permute-start.32
  851.4 19.4 %collective-permute-start.35 = (bf16[3,1,64,2048]{3,2,1,0:T(8,128)(2,1)S(1)}, bf16[3,1,64,2048]{3,2,1,0:T(8,128)(2,1)S(1)}, u32[]{:S(2)}, u32[]{:S(2)}) collective-permute-start(bf16[3,1,64,2048]{3,2,1,0:T(8,128)(2,1)S(1)} %pad_maximum_fusion.8), channel_id=1, source_target_pairs={{1,0},{2,1},{3,2},{4,3},{5,4},{6,5},{7,6},{9,8},{10,9},{11,10},{12... | collective-permute-start | bytes 2359304 | tf_op jit(solution)/shard_map/ppermute | solution.py:27
  861.9 10.8 collective-permute-start.34
  981.2 9.6 collective-permute-start.37
  982.5 9.2 collective-permute-start.36
  991.8 13.3 collective-permute-start.39
  995.0 11.3 collective-permute-start.38
  1058.3 7.1 collective-permute-start.41
  1059.6 7.3 collective-permute-start.40
  1067.0 19.4 %collective-permute-start.43 = (bf16[3,1,64,2048]{3,2,1,0:T(8,128)(2,1)S(1)}, bf16[3,1,64,2048]{3,2,1,0:T(8,128)(2,1)S(1)}, u32[]{:S(2)}, u32[]{:S(2)}) collective-permute-start(bf16[3,1,64,2048]{3,2,1,0:T(8,128)(2,1)S(1)} %pad_maximum_fusion.10), channel_id=1, source_target_pairs={{1,0},{2,1},{3,2},{4,3},{5,4},{6,5},{7,6},{9,8},{10,9},{11,10},{12... | collective-permute-start | bytes 2359304 | tf_op jit(solution)/shard_map/ppermute | solution.py:27
  1077.5 10.8 collective-permute-start.42
  1088.4 71.8 %copy-start.35 = (f32[64,512]{1,0:T(8,128)}, f32[64,512]{1,0:T(8,128)S(1)}, u32[]{:S(2)}) copy-start(f32[64,512]{1,0:T(8,128)S(1)} %get-tuple-element.12) | copy-start | bytes 393220
  1088.4 71.8 %copy-start.36 = (f32[64,512]{1,0:T(8,128)}, f32[64,512]{1,0:T(8,128)S(1)}, u32[]{:S(2)}) copy-start(f32[64,512]{1,0:T(8,128)S(1)} %get-tuple-element.13) | copy-start | bytes 393220
  1196.9 9.6 collective-permute-start.45
  1198.2 9.2 collective-permute-start.44
  1207.5 13.3 collective-permute-start.47
  1210.7 11.3 collective-permute-start.46
  1222.0 145.4 %copy-start.6 = (f32[64,512]{1,0:T(8,128)S(1)}, f32[64,512]{1,0:T(8,128)}, u32[]{:S(2)}) copy-start(f32[64,512]{1,0:T(8,128)} %copy-done.5) | copy-start | bytes 393220
  1222.0 145.4 %copy-start.8 = (f32[64,512]{1,0:T(8,128)S(1)}, f32[64,512]{1,0:T(8,128)}, u32[]{:S(2)}) copy-start(f32[64,512]{1,0:T(8,128)} %copy-done.7) | copy-start | bytes 393220
  1267.0 103.4 %copy-start.2 = (f32[64,512]{1,0:T(8,128)S(1)}, f32[64,512]{1,0:T(8,128)}, u32[]{:S(2)}) copy-start(f32[64,512]{1,0:T(8,128)} %copy-done.1) | copy-start | bytes 393220
  1267.0 103.4 %copy-start.4 = (f32[64,512]{1,0:T(8,128)S(1)}, f32[64,512]{1,0:T(8,128)}, u32[]{:S(2)}) copy-start(f32[64,512]{1,0:T(8,128)} %copy-done.3) | copy-start | bytes 393220
  1272.1 7.1 collective-permute-start.49
  1273.4 7.3 collective-permute-start.48
  1280.8 19.4 %collective-permute-start.51 = (bf16[3,1,64,2048]{3,2,1,0:T(8,128)(2,1)S(1)}, bf16[3,1,64,2048]{3,2,1,0:T(8,128)(2,1)S(1)}, u32[]{:S(2)}, u32[]{:S(2)}) collective-permute-start(bf16[3,1,64,2048]{3,2,1,0:T(8,128)(2,1)S(1)} %pad_maximum_fusion.12), channel_id=1, source_target_pairs={{1,0},{2,1},{3,2},{4,3},{5,4},{6,5},{7,6},{9,8},{10,9},{11,10},{12... | collective-permute-start | bytes 2359304 | tf_op jit(solution)/shard_map/ppermute | solution.py:27
  1291.2 10.8 collective-permute-start.50
  (35 other events, 1361.0 us)
